TPU v7x, 1024 devices: a whole 4x4x32 slice. The times are simulated.
1024 devices in a mesh: dp: 2 (over x_hi), outer: 128 (over z, x_lo, core), inner: 4 (over y).
Axes of the slice: x: 4 (x_hi: 2, x_lo: 2; x = x_hi * 2 + x_lo), y: 4, z: 32, core: 2. Of those that a mesh axis runs over, the one named last changes fastest.
Arguments:
- queries: bfloat16 [65536, 4096], P(('outer', 'inner'), 'dp'), may hold values from -512 to 512
- out_grad: bfloat16 [65536, 4096], P(('outer', 'inner'), 'dp'), may hold values from -6 to 6
- key_rows: bfloat16 [65536, 512], P(('outer', 'inner')), may hold values from -14 to 14
- value_rows: bfloat16 [65536, 512], P(('outer', 'inner')), may hold values from -6 to 6
- block_order: int32 [512], replicated, may hold values from 0 to 511, each once
- block_flags: int32 [512, 5], replicated, may hold values 0 or 1
Outputs:
- query_grad: bfloat16 [65536, 4096], P(('outer', 'inner'), 'dp')
- key_grad: float32 [65536, 512], P(('outer', 'inner'), 'dp')
- value_grad: float32 [65536, 512], P(('outer', 'inner'), 'dp')
Inputs may be any that keep to these rules, and one draw needn't show every extreme that they name: `block_order`: each number appears once.
All inputs are finite; a program needn't handle non-finite values.
Results may differ from a plain program's by a relative error of at most 0.005.
Values may be sent and summed in bfloat16 or wider, within the bound.
No kernel may reach another device: no remote copies, remote signals or barrier semaphores. Data moves between devices by JAX's collectives and lax.ppermute only.
A program may use at most 32 MiB of HBM per device.

v0:
```python
import functools
import math

import jax
import jax.numpy as jnp
from jax import lax
from jax.experimental import pallas as pl
from jax.experimental.pallas import tpu as pltpu
from jax.sharding import PartitionSpec as P


HD = 128
SCALE = 1.0 / math.sqrt(HD)
LOG2E = 1.4426950408889634
VMEM = pl.BlockSpec(memory_space=pltpu.VMEM)
SMEM = pl.BlockSpec(memory_space=pltpu.SMEM)
HBM = pl.BlockSpec(memory_space=pltpu.HBM)
BF = jnp.bfloat16
F32 = jnp.float32


def passed_along(x, axis, by):
    devices = lax.axis_size(axis)
    return lax.ppermute(x, axis, [(i, (i + by) % devices) for i in range(devices)])


def lanes(start, size):
    return pl.ds(pl.multiple_of(start, 128), size)


def stay(x):
    return pltpu.with_memory_space_constraint(x, pltpu.HBM)


def limit(mib):
    return pltpu.CompilerParams(vmem_limit_bytes=mib << 20)


def pack_kernel(dims, order_hbm, flag_hbm, q_ref, g_ref, k_ref, v_ref, send_ref, kv4_ref, kv_ref, bias_ref, order_ref, flag_ref, sems):
    groups, half, members, outers = dims
    rows = kv_ref.shape[0]
    d = lax.axis_index("dp")
    outer = lax.axis_index("outer")
    member = lax.axis_index("inner")
    wide = groups * half
    moves = [(order_hbm, order_ref), (flag_hbm, flag_ref)]
    for base, ref in ((0, k_ref), (half, v_ref)):
        source = ref.at[:, lanes(d * half, half)]
        moves.append((source, kv_ref.at[:, base : base + half]))
    for g in range(groups):
        away = g * 2 * half + (1 - d) * half
        for base, ref in ((0, q_ref), (wide, g_ref)):
            at = base + g * half
            moves.append((ref.at[:, lanes(away, half)], send_ref.at[:, at : at + half]))
    for c in range(members):
        moves.append((kv_ref, kv4_ref.at[c * rows : (c + 1) * rows, :]))
    copies = [pltpu.make_async_copy(a, b, sems.at[i]) for i, (a, b) in enumerate(moves)]
    for copy in copies[:-members]:
        copy.start()
    copies[2].wait()
    copies[3].wait()
    for copy in copies[-members:]:
        copy.start()
    copies[0].wait()
    copies[1].wait()
    shard = outer * members + member
    before = lax.rem(outer + outers - 1, outers) * members + member
    mine = order_ref[shard]
    key_at = lax.broadcasted_iota(jnp.int32, (rows, rows), 0)
    row_at = lax.broadcasted_iota(jnp.int32, (rows, rows), 1)
    triangle = jnp.where(key_at <= row_at, 0.0, -jnp.inf).astype(F32)
    for c in range(members + 1):
        where = outer * members + c if c < members else before
        seen = jnp.logical_and(order_ref[where] < mine, flag_ref[c, shard] == 1)
        flat = jnp.full((rows, rows), jnp.where(seen, 0.0, -jnp.inf), F32)
        if c < members:
            flat = jnp.where(member == c, triangle, flat)
        bias_ref[c * rows : (c + 1) * rows, :] = flat
    for copy in copies[4:]:
        copy.wait()


def attend_kernel(half, groups, members, q_ref, g_ref, qg_ref, kv_ref, prev_ref, bias_ref, own_dq, far_dq, part_ref, back_ref, *scratch):
    scores, grads, softs, slopes = scratch[0:2], scratch[2:4], scratch[4:6], scratch[6:8]
    keys_t, key_sum, value_sum, part_vmem, sems = scratch[8:13]
    copies = []
    rows = prev_ref.shape[0]
    slots = members + 1
    per = half // HD
    wide = groups * half
    d = lax.axis_index("dp")
    nt = (((1,), (1,)), ((), ()))
    units = [(j, own, g) for j in range(per) for own in (True, False) for g in range(0, groups, 2)]
    pack = groups // 2

    def chunk(j, c, base):
        if c == members:
            return prev_ref[:, base + j * HD : base + (j + 1) * HD]
        return kv_ref[c * rows : (c + 1) * rows, base + j * HD : base + (j + 1) * HD]

    def heads(i, grad):
        j, own, g = units[i]
        if own:
            ref = g_ref if grad else q_ref
            parts = [ref[:, lanes((g + e) * 2 * half + d * half + j * HD, HD)] for e in range(2)]
        else:
            base = wide if grad else 0
            parts = [qg_ref[:, base + (g + e) * half + j * HD : base + (g + e) * half + (j + 1) * HD] for e in range(2)]
        return jnp.concatenate(parts, 0)

    def fold(x, op):
        return op(x.reshape(x.shape[0] // 8, 8, x.shape[1]), axis=0)

    def stage_a(i):
        j = units[i][0]
        q2, g2 = heads(i, False), heads(i, True)
        span = members * rows
        tops = []
        for at, ref in ((slice(0, span), kv_ref), (slice(span, span + rows), prev_ref)):
            bias = bias_ref[at, :]
            s = lax.dot_general(ref[:, j * HD : (j + 1) * HD], q2, nt, preferred_element_type=F32)
            s = s + jnp.concatenate([bias, bias], 1)
            scores[i % 2][at, :] = s
            tops.append(fold(s, jnp.max))
            lane = slice(half + j * HD, half + (j + 1) * HD)
            grads[i % 2][at, :] = lax.dot_general(ref[:, lane], g2, nt, preferred_element_type=F32)
        return jnp.max(jnp.maximum(*tops), axis=0, keepdims=True)

    def stage_b(i, top):
        total = delta = None
        for c in range(slots):
            at = slice(c * rows, (c + 1) * rows)
            e = jnp.exp2((scores[i % 2][at, :] - top) * (SCALE * LOG2E))
            scores[i % 2][at, :] = e
            te, de = fold(e, jnp.sum), fold(e * grads[i % 2][at, :], jnp.sum)
            total = te if total is None else total + te
            delta = de if delta is None else delta + de
        inverse = 1.0 / jnp.sum(total, axis=0, keepdims=True)
        delta = jnp.sum(delta, axis=0, keepdims=True) * inverse
        bunch, lane = (i // pack) % 2, (i % pack) * 2 * rows
        for c in range(slots):
            at = slice(c * rows, (c + 1) * rows)
            soft = scores[i % 2][at, :] * inverse
            softs[bunch][at, lane : lane + 2 * rows] = soft.astype(BF)
            slope = soft * ((grads[i % 2][at, :] - delta) * SCALE)
            slopes[bunch][at, lane : lane + 2 * rows] = slope.astype(BF)

    def stage_q(i):
        j, own, g = units[i]
        bunch, lane = (i // pack) % 2, (i % pack) * 2 * rows
        out = jnp.dot(keys_t[j], slopes[bunch][:, lane : lane + 2 * rows], preferred_element_type=F32)
        ref = own_dq if own else far_dq
        for e in range(2):
            at = (g + e) * half + j * HD
            ref[:, at : at + HD] = out[:, e * rows : (e + 1) * rows].T.astype(BF)

    def stage_kv(k, grad):
        first = k * pack
        j, own, _ = units[first]
        other = jnp.concatenate([heads(first + e, grad) for e in range(pack)], 0)
        weights, total, base = (softs, value_sum, half) if grad else (slopes, key_sum, 0)
        out = jnp.dot(weights[k % 2][...], other, preferred_element_type=F32)
        if own:
            total[...] = out
            return
        out = (total[...] + out).astype(BF)
        lane = slice(base + j * HD, base + (j + 1) * HD)
        part_vmem[:, lane] = out[: members * rows]
        back_ref[:, lane] = out[members * rows :]
        copies.append(pltpu.make_async_copy(part_vmem.at[:, lane], part_ref.at[:, lane], sems.at[len(copies)]))
        copies[-1].start()

    for j in range(per):
        for c in range(slots):
            at = slice(c * rows, (c + 1) * rows)
            keys_t[j, :, at] = chunk(j, c, 0).T
    count = len(units)
    tops = {}
    for t in range(count + pack + 2):
        if 0 <= t - 1 < count:
            stage_b(t - 1, tops.pop(t - 1))
        if t < count:
            tops[t] = stage_a(t)
        for lag, grad in ((pack, True), (pack + 1, False)):
            k, rest = divmod(t - lag - 1, pack)
            if rest == 0 and 0 <= k < count // pack:
                stage_kv(k, grad)
        if 0 <= t - 2 < count:
            stage_q(t - 2)
    for copy in copies:
        copy.wait()


def finish_kernel(half, groups, members, part_ref, back_ref, own_dq_ref, far_dq_ref, dq_ref, dk_ref, dv_ref):
    rows = back_ref.shape[0]
    d = lax.axis_index("dp")
    for g in range(groups):
        dq_ref[:, lanes(g * 2 * half + d * half, half)] = own_dq_ref[:, g * half : (g + 1) * half]
        dq_ref[:, lanes(g * 2 * half + (1 - d) * half, half)] = far_dq_ref[:, g * half : (g + 1) * half]
    total = back_ref[...].astype(F32)
    for c in range(members):
        total = total + part_ref[c * rows : (c + 1) * rows, :].astype(F32)
    dk_ref[...] = total[:, :half]
    dv_ref[...] = total[:, half:]


def step(queries, out_grad, key_rows, value_rows, block_order, block_flags):
    rows = queries.shape[0]
    key_heads = key_rows.shape[1] // HD
    groups = queries.shape[1] // (key_heads * HD)
    members = lax.axis_size("inner")
    outers = lax.axis_size("outer")
    half = key_heads * HD // lax.axis_size("dp")
    per = half // HD
    window = (members + 1) * rows
    S = jax.ShapeDtypeStruct
    send, kv4, kv, bias = pl.pallas_call(
        functools.partial(pack_kernel, (groups, half, members, outers)),
        out_shape=(
            S((rows, 2 * groups * half), BF),
            S((members * rows, 2 * half), BF),
            S((rows, 2 * half), BF),
            S((window, rows), F32),
        ),
        in_specs=[HBM] * 6,
        out_specs=(VMEM, HBM, VMEM, VMEM),
        scratch_shapes=[
            pltpu.SMEM(block_order.shape, jnp.int32),
            pltpu.SMEM(block_flags.shape[::-1], jnp.int32),
            pltpu.SemaphoreType.DMA((4 + 2 * groups + members,)),
        ],
        compiler_params=limit(8),
        name="pack",
    )(*[stay(a) for a in (block_order, block_flags.T, queries, out_grad, key_rows, value_rows)])
    prev_kv = passed_along(kv, "outer", 1)
    received = passed_along(send, "dp", 1)
    group_kv = lax.all_to_all(kv4, "inner", 0, 0, tiled=True)
    cost = pl.CostEstimate(
        flops=20 * rows * window * HD * groups * per,
        transcendentals=2 * rows * window * groups * per,
        bytes_accessed=8 * rows * window * per * groups,
    )
    own_dq, far_dq, part, back = pl.pallas_call(
        functools.partial(attend_kernel, half, groups, members),
        out_shape=(
            S((rows, groups * half), BF),
            S((rows, groups * half), BF),
            S((members * rows, 2 * half), BF),
            S((rows, 2 * half), BF),
        ),
        in_specs=[VMEM] * 6,
        out_specs=(VMEM, VMEM, HBM, VMEM),
        scratch_shapes=[pltpu.VMEM((window, 2 * rows), F32)] * 4
        + [pltpu.VMEM((window, groups * rows), BF)] * 4
        + [pltpu.VMEM((per, HD, window), BF), pltpu.VMEM((window, HD), F32), pltpu.VMEM((window, HD), F32)]
        + [pltpu.VMEM((members * rows, 2 * half), BF), pltpu.SemaphoreType.DMA((2 * per,))],
        cost_estimate=cost,
        compiler_params=pltpu.CompilerParams(vmem_limit_bytes=24 << 20),
        name="attend",
    )(queries, out_grad, received, group_kv, prev_kv, bias)
    far_dq = passed_along(far_dq, "dp", 1)
    part = lax.all_to_all(part, "inner", 0, 0, tiled=True)
    back = passed_along(back, "outer", -1)
    return pl.pallas_call(
        functools.partial(finish_kernel, half, groups, members),
        out_shape=(S(queries.shape, BF), S((rows, half), F32), S((rows, half), F32)),
        in_specs=[VMEM] * 4,
        out_specs=(VMEM,) * 3,
        compiler_params=limit(8),
        name="finish",
    )(part, back, own_dq, far_dq)


def solution(mesh):
    tokens = P(("outer", "inner"), None)
    split = P(("outer", "inner"), "dp")
    return jax.shard_map(
        step,
        mesh=mesh,
        in_specs=(split, split, tokens, tokens, P(), P()),
        out_specs=(split, split, split),
        check_vma=False,
    )
```

profile of v0, /device:TPU:8, one launch (start us, length us, event | category | flops | bytes accessed | tf_op | source)
XLA Modules:
  0.0 56.3 jit_solution(6012362574490348529)
XLA Ops:
  0.6 1.8 %pack.1 = (bf16[128,2048]{1,0:T(8,128)(2,1)S(1)}, bf16[512,512]{1,0:T(8,128)(2,1)}, bf16[128,512]{1,0:T(8,128)(2,1)S(1)}, f32[640,128]{1,0:T(8,128)S(1)}) custom-call(s32[512]{0:T(512)} %order_hbm.1, s32[5,512]{1,0:T(8,128)} %bitcast.7, bf16[128,2048]{1,0:T(8,128)(2,1)} %q_ref.3, bf16[128,2048]{1,0:T(8,128)(2,1)} %g_ref.3, bf16[128,512]{1,0:T(8,128)(2,1)} %k_ref.1, ...), custom_call_target="tpu_custom_call" | custom-call | tf_op jit(solution)/shard_map/pack/pallas_call | solution.py:217
  2.4 4.9 %collective-permute-start = (bf16[128,2048]{1,0:T(8,128)(2,1)S(1)}, bf16[128,2048]{1,0:T(8,128)(2,1)S(1)}, u32[]{:S(2)}, u32[]{:S(2)}) collective-permute-start(bf16[128,2048]{1,0:T(8,128)(2,1)S(1)} %get-tuple-element.11), channel_id=1, source_target_pairs={{0,512},{512,0},{1,513},{513,1},{2,514},{514,2},{3,515},{515,3},{4... | collective-permute-start | bytes 1572872 | tf_op jit(solution)/shard_map/ppermute | solution.py:24
  7.4 0.0 copy-start
  7.4 0.0 copy-start.1
  7.4 13.6 %all-to-all-start = ((bf16[4,128,512]{2,1,0:T(8,128)(2,1)}), bf16[4,128,512]{2,1,0:T(8,128)(2,1)S(1)}, u32[]{:S(2)}, u32[]{:S(2)}) async-start(bf16[4,128,512]{2,1,0:T(8,128)(2,1)} %bitcast.1), calls=%async_computation | async-start | bytes 1048576 | tf_op jit(solution)/shard_map/all_to_all | solution.py:237
  21.1 1.9 %collective-permute-start.1 = (bf16[128,512]{1,0:T(8,128)(2,1)S(1)}, bf16[128,512]{1,0:T(8,128)(2,1)S(1)}, u32[]{:S(2)}, u32[]{:S(2)}) collective-permute-start(bf16[128,512]{1,0:T(8,128)(2,1)S(1)} %get-tuple-element.13), channel_id=1, source_target_pairs={{0,4},{4,8},{8,12},{12,16},{16,20},{20,24},{24,28},{28,32},{32,36}... | collective-permute-start | bytes 393224 | tf_op jit(solution)/shard_map/ppermute | solution.py:24
  23.0 9.4 %collective-permute-done.1.prev_ref = bf16[128,512]{1,0:T(8,128)(2,1)S(1)} collective-permute-done((bf16[128,512]{1,0:T(8,128)(2,1)S(1)}, bf16[128,512]{1,0:T(8,128)(2,1)S(1)}, u32[]{:S(2)}, u32[]{:S(2)}) %collective-permute-start.1) | collective-permute-done | bytes 131104 | tf_op jit(solution)/shard_map/ppermute | solution.py:24
  32.4 0.0 all-to-all-done
  32.4 0.0 collective-permute-done.qg_ref
  32.4 0.0 copy-done
  32.4 0.0 copy-done.1
  32.4 5.6 %attend.1 = (bf16[128,1024]{1,0:T(8,128)(2,1)S(1)}, bf16[128,1024]{1,0:T(8,128)(2,1)S(1)}, bf16[512,512]{1,0:T(8,128)(2,1)}, bf16[128,512]{1,0:T(8,128)(2,1)S(1)}) custom-call(bf16[128,2048]{1,0:T(8,128)(2,1)S(1)} %copy-done, bf16[128,2048]{1,0:T(8,128)(2,1)S(1)} %copy-done.1, bf16[128,2048]{1,0:T(8,128)(2,1)S(1)} %collective-permute-done.qg_ref, ...), custom_call_target="tpu_custom_call" | custom-call | flops 1677721600 | bytes 5242880 | tf_op jit(solution)/shard_map/attend/pallas_call | solution.py:243
  38.0 4.8 %all-to-all-start.1 = ((bf16[4,128,512]{2,1,0:T(8,128)(2,1)}), bf16[4,128,512]{2,1,0:T(8,128)(2,1)S(1)}, u32[]{:S(2)}, u32[]{:S(2)}) async-start(bf16[4,128,512]{2,1,0:T(8,128)(2,1)} %bitcast.3), calls=%async_computation.1 | async-start | bytes 1048576 | tf_op jit(solution)/shard_map/all_to_all | solution.py:262
  42.9 3.9 %collective-permute-start.3 = (bf16[128,1024]{1,0:T(8,128)(2,1)S(1)}, bf16[128,1024]{1,0:T(8,128)(2,1)S(1)}, u32[]{:S(2)}, u32[]{:S(2)}) collective-permute-start(bf16[128,1024]{1,0:T(8,128)(2,1)S(1)} %get-tuple-element.18), channel_id=1, source_target_pairs={{0,512},{512,0},{1,513},{513,1},{2,514},{514,2},{3,515},{515,3},{4... | collective-permute-start | bytes 786440 | tf_op jit(solution)/shard_map/ppermute | solution.py:24
  46.8 6.1 %collective-permute-start.2 = (bf16[128,512]{1,0:T(8,128)(2,1)S(1)}, bf16[128,512]{1,0:T(8,128)(2,1)S(1)}, u32[]{:S(2)}, u32[]{:S(2)}) collective-permute-start(bf16[128,512]{1,0:T(8,128)(2,1)S(1)} %get-tuple-element.16), channel_id=1, source_target_pairs={{0,508},{4,0},{8,4},{12,8},{16,12},{20,16},{24,20},{28,24},{32,28}... | collective-permute-start | bytes 393224 | tf_op jit(solution)/shard_map/ppermute | solution.py:24
  52.9 2.5 %collective-permute-done.2.back_ref = bf16[128,512]{1,0:T(8,128)(2,1)S(1)} collective-permute-done((bf16[128,512]{1,0:T(8,128)(2,1)S(1)}, bf16[128,512]{1,0:T(8,128)(2,1)S(1)}, u32[]{:S(2)}, u32[]{:S(2)}) %collective-permute-start.2) | collective-permute-done | bytes 131104 | tf_op jit(solution)/shard_map/ppermute | solution.py:24
  55.4 0.0 collective-permute-done.3.far_dq_ref
  55.4 0.0 all-to-all-done.1
  55.4 1.0 %finish.1 = (bf16[128,2048]{1,0:T(8,128)(2,1)}, f32[128,256]{1,0:T(8,128)}, f32[128,256]{1,0:T(8,128)}) custom-call(bf16[512,512]{1,0:T(8,128)(2,1)S(1)} %bitcast.5, bf16[128,512]{1,0:T(8,128)(2,1)S(1)} %collective-permute-done.2.back_ref, bf16[128,1024]{1,0:T(8,128)(2,1)S(1)} %get-tuple-element.17.own_dq_ref, ...), custom_call_target="tpu_custom_call" | custom-call | tf_op jit(solution)/shard_map/finish/pallas_call | solution.py:264
Async XLA Ops:
  2.4 30.0 %collective-permute-start = (bf16[128,2048]{1,0:T(8,128)(2,1)S(1)}, bf16[128,2048]{1,0:T(8,128)(2,1)S(1)}, u32[]{:S(2)}, u32[]{:S(2)}) collective-permute-start(bf16[128,2048]{1,0:T(8,128)(2,1)S(1)} %get-tuple-element.11), channel_id=1, source_target_pairs={{0,512},{512,0},{1,513},{513,1},{2,514},{514,2},{3,515},{515,3},{4... | collective-permute-start | bytes 1572872 | tf_op jit(solution)/shard_map/ppermute | solution.py:24
  7.4 25.0 %copy-start = (bf16[128,2048]{1,0:T(8,128)(2,1)S(1)}, bf16[128,2048]{1,0:T(8,128)(2,1)}, u32[]{:S(2)}) copy-start(bf16[128,2048]{1,0:T(8,128)(2,1)} %q_ref.3) | copy-start | bytes 1572868
  7.4 25.0 %copy-start.1 = (bf16[128,2048]{1,0:T(8,128)(2,1)S(1)}, bf16[128,2048]{1,0:T(8,128)(2,1)}, u32[]{:S(2)}) copy-start(bf16[128,2048]{1,0:T(8,128)(2,1)} %g_ref.3) | copy-start | bytes 1572868
  7.4 25.0 %all-to-all-start = ((bf16[4,128,512]{2,1,0:T(8,128)(2,1)}), bf16[4,128,512]{2,1,0:T(8,128)(2,1)S(1)}, u32[]{:S(2)}, u32[]{:S(2)}) async-start(bf16[4,128,512]{2,1,0:T(8,128)(2,1)} %bitcast.1), calls=%async_computation | async-start | bytes 1048576 | tf_op jit(solution)/shard_map/all_to_all | solution.py:237
  21.1 11.4 %collective-permute-start.1 = (bf16[128,512]{1,0:T(8,128)(2,1)S(1)}, bf16[128,512]{1,0:T(8,128)(2,1)S(1)}, u32[]{:S(2)}, u32[]{:S(2)}) collective-permute-start(bf16[128,512]{1,0:T(8,128)(2,1)S(1)} %get-tuple-element.13), channel_id=1, source_target_pairs={{0,4},{4,8},{8,12},{12,16},{16,20},{20,24},{24,28},{28,32},{32,36}... | collective-permute-start | bytes 393224 | tf_op jit(solution)/shard_map/ppermute | solution.py:24
  38.0 17.3 %all-to-all-start.1 = ((bf16[4,128,512]{2,1,0:T(8,128)(2,1)}), bf16[4,128,512]{2,1,0:T(8,128)(2,1)S(1)}, u32[]{:S(2)}, u32[]{:S(2)}) async-start(bf16[4,128,512]{2,1,0:T(8,128)(2,1)} %bitcast.3), calls=%async_computation.1 | async-start | bytes 1048576 | tf_op jit(solution)/shard_map/all_to_all | solution.py:262
  42.9 12.5 %collective-permute-start.3 = (bf16[128,1024]{1,0:T(8,128)(2,1)S(1)}, bf16[128,1024]{1,0:T(8,128)(2,1)S(1)}, u32[]{:S(2)}, u32[]{:S(2)}) collective-permute-start(bf16[128,1024]{1,0:T(8,128)(2,1)S(1)} %get-tuple-element.18), channel_id=1, source_target_pairs={{0,512},{512,0},{1,513},{513,1},{2,514},{514,2},{3,515},{515,3},{4... | collective-permute-start | bytes 786440 | tf_op jit(solution)/shard_map/ppermute | solution.py:24
  46.8 8.6 %collective-permute-start.2 = (bf16[128,512]{1,0:T(8,128)(2,1)S(1)}, bf16[128,512]{1,0:T(8,128)(2,1)S(1)}, u32[]{:S(2)}, u32[]{:S(2)}) collective-permute-start(bf16[128,512]{1,0:T(8,128)(2,1)S(1)} %get-tuple-element.16), channel_id=1, source_target_pairs={{0,508},{4,0},{8,4},{12,8},{16,12},{20,16},{24,20},{28,24},{32,28}... | collective-permute-start | bytes 393224 | tf_op jit(solution)/shard_map/ppermute | solution.py:24
where the time goes:
time: 56.7 us; the launch traced here: 56.3 us
  starting transfers between devices  35.3 us (62%)
  waiting for transfers between devices  11.9 us (21%)
  Pallas kernels  8.38 us (15%)
  between operations  0.71 us (1%)
    ppermute x4, starting transfers between devices, passed_along(): lax.ppermute(x, axis, [(i, (i + by) % devices) for i in range(devices)])  16.8 us
    all_to_all x1, starting transfers between devices, step(): group_kv = lax.all_to_all(kv4, 'inner', 0, 0, tiled=True)  13.6 us
    ppermute x4, waiting for transfers between devices, passed_along(): lax.ppermute(x, axis, [(i, (i + by) % devices) for i in range(devices)])  11.9 us
    pallas_call x1, Pallas kernels, step(): pl.pallas_call(functools.partial(attend_kernel, half, groups, members), o...  5.61 us
    all_to_all x1, starting transfers between devices, step(): part = lax.all_to_all(part, 'inner', 0, 0, tiled=True)  4.81 us
    pallas_call x1, Pallas kernels, step(): pl.pallas_call(functools.partial(pack_kernel, (groups, half, members, out...  1.81 us
  transfers between devices with their start and end apart: 6, of which 2 were waited for; matrix products, arithmetic and copies ran while one was open for 0% of the time, Pallas kernels for 0%

commit v1 on v0

--- a/solution.py
+++ b/solution.py
@@ -36,7 +36,7 @@
     return pltpu.CompilerParams(vmem_limit_bytes=mib << 20)
 
 
-def pack_kernel(dims, order_hbm, flag_hbm, q_ref, g_ref, k_ref, v_ref, send_ref, kv4_ref, kv_ref, bias_ref, order_ref, flag_ref, sems):
+def pack_kernel(dims, order_hbm, flag_hbm, q_ref, g_ref, k_ref, v_ref, send_ref, kv_ref, bias_ref, order_ref, flag_ref, sems):
     groups, half, members, outers = dims
     rows = kv_ref.shape[0]
     d = lax.axis_index("dp")
@@ -52,14 +52,8 @@
         for base, ref in ((0, q_ref), (wide, g_ref)):
             at = base + g * half
             moves.append((ref.at[:, lanes(away, half)], send_ref.at[:, at : at + half]))
-    for c in range(members):
-        moves.append((kv_ref, kv4_ref.at[c * rows : (c + 1) * rows, :]))
     copies = [pltpu.make_async_copy(a, b, sems.at[i]) for i, (a, b) in enumerate(moves)]
-    for copy in copies[:-members]:
-        copy.start()
-    copies[2].wait()
-    copies[3].wait()
-    for copy in copies[-members:]:
+    for copy in copies:
         copy.start()
     copies[0].wait()
     copies[1].wait()
@@ -76,7 +70,18 @@
         if c < members:
             flat = jnp.where(member == c, triangle, flat)
         bias_ref[c * rows : (c + 1) * rows, :] = flat
-    for copy in copies[4:]:
+    for copy in copies[2:]:
+        copy.wait()
+
+
+def spread_kernel(members, kv_ref, kv4_ref, sems):
+    rows = kv_ref.shape[0]
+    copies = [
+        pltpu.make_async_copy(kv_ref, kv4_ref.at[c * rows : (c + 1) * rows, :], sems.at[c]) for c in range(members)
+    ]
+    for copy in copies:
+        copy.start()
+    for copy in copies:
         copy.wait()
 
 
@@ -214,26 +219,34 @@
     per = half // HD
     window = (members + 1) * rows
     S = jax.ShapeDtypeStruct
-    send, kv4, kv, bias = pl.pallas_call(
+    send, kv, bias = pl.pallas_call(
         functools.partial(pack_kernel, (groups, half, members, outers)),
         out_shape=(
             S((rows, 2 * groups * half), BF),
-            S((members * rows, 2 * half), BF),
             S((rows, 2 * half), BF),
             S((window, rows), F32),
         ),
         in_specs=[HBM] * 6,
-        out_specs=(VMEM, HBM, VMEM, VMEM),
+        out_specs=(VMEM,) * 3,
         scratch_shapes=[
             pltpu.SMEM(block_order.shape, jnp.int32),
             pltpu.SMEM(block_flags.shape[::-1], jnp.int32),
-            pltpu.SemaphoreType.DMA((4 + 2 * groups + members,)),
+            pltpu.SemaphoreType.DMA((4 + 2 * groups,)),
         ],
         compiler_params=limit(8),
         name="pack",
     )(*[stay(a) for a in (block_order, block_flags.T, queries, out_grad, key_rows, value_rows)])
     prev_kv = passed_along(kv, "outer", 1)
     received = passed_along(send, "dp", 1)
+    kv4 = pl.pallas_call(
+        functools.partial(spread_kernel, members),
+        out_shape=S((members * rows, 2 * half), BF),
+        in_specs=[VMEM],
+        out_specs=HBM,
+        scratch_shapes=[pltpu.SemaphoreType.DMA((members,))],
+        compiler_params=limit(4),
+        name="spread",
+    )(kv)
     group_kv = lax.all_to_all(kv4, "inner", 0, 0, tiled=True)
     cost = pl.CostEstimate(
         flops=20 * rows * window * HD * groups * per,

time: 56.7 us -> 55.1 us (0.972)
  the two profiles are of different devices: /device:TPU:8 before, /device:TPU:12 now
where the time goes in v1:
time: 55.1 us; the launch traced here: 54.7 us
  starting transfers between devices  34.9 us (63%)
  waiting for transfers between devices  10.4 us (19%)
  Pallas kernels  8.66 us (16%)
  between operations  0.72 us (1%)
    all_to_all x1, starting transfers between devices, step(): group_kv = lax.all_to_all(kv4, 'inner', 0, 0, tiled=True)  16.7 us
    ppermute x4, starting transfers between devices, passed_along(): lax.ppermute(x, axis, [(i, (i + by) % devices) for i in range(devices)])  13.4 us
    ppermute x4, waiting for transfers between devices, passed_along(): lax.ppermute(x, axis, [(i, (i + by) % devices) for i in range(devices)])  10.4 us
    pallas_call x1, Pallas kernels, step(): pl.pallas_call(functools.partial(attend_kernel, half, groups, members), o...  5.64 us
    all_to_all x1, starting transfers between devices, step(): part = lax.all_to_all(part, 'inner', 0, 0, tiled=True)  4.81 us
    pallas_call x1, Pallas kernels, step(): pl.pallas_call(functools.partial(pack_kernel, (groups, half, members, out...  1.24 us
  transfers between devices with their start and end apart: 6, of which 2 were waited for; matrix products, arithmetic and copies ran while one was open for 0% of the time, Pallas kernels for 2%

profile of v1, /device:TPU:12, one launch (start us, length us, event | category | flops | bytes accessed | tf_op | source)
XLA Modules:
  0.0 54.7 jit_solution(11891107249011680599)
XLA Ops:
  0.6 1.2 %pack.1 = (bf16[128,2048]{1,0:T(8,128)(2,1)S(1)}, bf16[128,512]{1,0:T(8,128)(2,1)S(1)}, f32[640,128]{1,0:T(8,128)S(1)}) custom-call(s32[512]{0:T(512)} %order_hbm.1, s32[5,512]{1,0:T(8,128)} %bitcast.7, bf16[128,2048]{1,0:T(8,128)(2,1)} %q_ref.3, bf16[128,2048]{1,0:T(8,128)(2,1)} %g_ref.3, bf16[128,512]{1,0:T(8,128)(2,1)} %k_ref.1, bf16[128,512]{1,0:T(8,128)(2,1)} %v_ref.1), custom_call_target="tpu_custom_call" | custom-call | tf_op jit(solution)/shard_map/pack/pallas_call | solution.py:222
  1.9 2.4 %collective-permute-start = (bf16[128,2048]{1,0:T(8,128)(2,1)S(1)}, bf16[128,2048]{1,0:T(8,128)(2,1)S(1)}, u32[]{:S(2)}, u32[]{:S(2)}) collective-permute-start(bf16[128,2048]{1,0:T(8,128)(2,1)S(1)} %get-tuple-element.10), channel_id=1, source_target_pairs={{0,512},{512,0},{1,513},{513,1},{2,514},{514,2},{3,515},{515,3},{4... | collective-permute-start | bytes 1572872 | tf_op jit(solution)/shard_map/ppermute | solution.py:24
  4.3 0.8 %spread.1 = bf16[512,512]{1,0:T(8,128)(2,1)} custom-call(bf16[128,512]{1,0:T(8,128)(2,1)S(1)} %get-tuple-element.11.kv_ref), custom_call_target="tpu_custom_call" | custom-call | tf_op jit(solution)/shard_map/spread/pallas_call | solution.py:241
  5.1 0.0 copy-start
  5.1 0.0 copy-start.1
  5.2 16.7 %all-to-all-start = ((bf16[4,128,512]{2,1,0:T(8,128)(2,1)}), bf16[4,128,512]{2,1,0:T(8,128)(2,1)S(1)}, u32[]{:S(2)}, u32[]{:S(2)}) async-start(bf16[4,128,512]{2,1,0:T(8,128)(2,1)} %bitcast.1), calls=%async_computation | async-start | bytes 1048576 | tf_op jit(solution)/shard_map/all_to_all | solution.py:250
  21.8 1.9 %collective-permute-start.1 = (bf16[128,512]{1,0:T(8,128)(2,1)S(1)}, bf16[128,512]{1,0:T(8,128)(2,1)S(1)}, u32[]{:S(2)}, u32[]{:S(2)}) collective-permute-start(bf16[128,512]{1,0:T(8,128)(2,1)S(1)} %get-tuple-element.11.kv_ref), channel_id=1, source_target_pairs={{0,4},{4,8},{8,12},{12,16},{16,20},{20,24},{24,28},{28,32},{32,36}... | collective-permute-start | bytes 393224 | tf_op jit(solution)/shard_map/ppermute | solution.py:24
  23.7 7.9 %collective-permute-done.1.prev_ref = bf16[128,512]{1,0:T(8,128)(2,1)S(1)} collective-permute-done((bf16[128,512]{1,0:T(8,128)(2,1)S(1)}, bf16[128,512]{1,0:T(8,128)(2,1)S(1)}, u32[]{:S(2)}, u32[]{:S(2)}) %collective-permute-start.1) | collective-permute-done | bytes 131104 | tf_op jit(solution)/shard_map/ppermute | solution.py:24
  31.7 0.0 all-to-all-done
  31.7 0.0 collective-permute-done.qg_ref
  31.7 0.0 copy-done
  31.7 0.0 copy-done.1
  31.7 5.6 %attend.1 = (bf16[128,1024]{1,0:T(8,128)(2,1)S(1)}, bf16[128,1024]{1,0:T(8,128)(2,1)S(1)}, bf16[512,512]{1,0:T(8,128)(2,1)}, bf16[128,512]{1,0:T(8,128)(2,1)S(1)}) custom-call(bf16[128,2048]{1,0:T(8,128)(2,1)S(1)} %copy-done, bf16[128,2048]{1,0:T(8,128)(2,1)S(1)} %copy-done.1, bf16[128,2048]{1,0:T(8,128)(2,1)S(1)} %collective-permute-done.qg_ref, ...), custom_call_target="tpu_custom_call" | custom-call | flops 1677721600 | bytes 5242880 | tf_op jit(solution)/shard_map/attend/pallas_call | solution.py:256
  37.3 4.8 %all-to-all-start.1 = ((bf16[4,128,512]{2,1,0:T(8,128)(2,1)}), bf16[4,128,512]{2,1,0:T(8,128)(2,1)S(1)}, u32[]{:S(2)}, u32[]{:S(2)}) async-start(bf16[4,128,512]{2,1,0:T(8,128)(2,1)} %bitcast.3), calls=%async_computation.1 | async-start | bytes 1048576 | tf_op jit(solution)/shard_map/all_to_all | solution.py:275
  42.1 3.4 %collective-permute-start.3 = (bf16[128,1024]{1,0:T(8,128)(2,1)S(1)}, bf16[128,1024]{1,0:T(8,128)(2,1)S(1)}, u32[]{:S(2)}, u32[]{:S(2)}) collective-permute-start(bf16[128,1024]{1,0:T(8,128)(2,1)S(1)} %get-tuple-element.16), channel_id=1, source_target_pairs={{0,512},{512,0},{1,513},{513,1},{2,514},{514,2},{3,515},{515,3},{4... | collective-permute-start | bytes 786440 | tf_op jit(solution)/shard_map/ppermute | solution.py:24
  45.5 5.7 %collective-permute-start.2 = (bf16[128,512]{1,0:T(8,128)(2,1)S(1)}, bf16[128,512]{1,0:T(8,128)(2,1)S(1)}, u32[]{:S(2)}, u32[]{:S(2)}) collective-permute-start(bf16[128,512]{1,0:T(8,128)(2,1)S(1)} %get-tuple-element.14), channel_id=1, source_target_pairs={{0,508},{4,0},{8,4},{12,8},{16,12},{20,16},{24,20},{28,24},{32,28}... | collective-permute-start | bytes 393224 | tf_op jit(solution)/shard_map/ppermute | solution.py:24
  51.3 2.5 %collective-permute-done.2.back_ref = bf16[128,512]{1,0:T(8,128)(2,1)S(1)} collective-permute-done((bf16[128,512]{1,0:T(8,128)(2,1)S(1)}, bf16[128,512]{1,0:T(8,128)(2,1)S(1)}, u32[]{:S(2)}, u32[]{:S(2)}) %collective-permute-start.2) | collective-permute-done | bytes 131104 | tf_op jit(solution)/shard_map/ppermute | solution.py:24
  53.8 0.0 collective-permute-done.3.far_dq_ref
  53.8 0.0 all-to-all-done.1
  53.8 1.0 %finish.1 = (bf16[128,2048]{1,0:T(8,128)(2,1)}, f32[128,256]{1,0:T(8,128)}, f32[128,256]{1,0:T(8,128)}) custom-call(bf16[512,512]{1,0:T(8,128)(2,1)S(1)} %bitcast.5, bf16[128,512]{1,0:T(8,128)(2,1)S(1)} %collective-permute-done.2.back_ref, bf16[128,1024]{1,0:T(8,128)(2,1)S(1)} %get-tuple-element.15.own_dq_ref, ...), custom_call_target="tpu_custom_call" | custom-call | tf_op jit(solution)/shard_map/finish/pallas_call | solution.py:277
Async XLA Ops:
  1.9 29.8 %collective-permute-start = (bf16[128,2048]{1,0:T(8,128)(2,1)S(1)}, bf16[128,2048]{1,0:T(8,128)(2,1)S(1)}, u32[]{:S(2)}, u32[]{:S(2)}) collective-permute-start(bf16[128,2048]{1,0:T(8,128)(2,1)S(1)} %get-tuple-element.10), channel_id=1, source_target_pairs={{0,512},{512,0},{1,513},{513,1},{2,514},{514,2},{3,515},{515,3},{4... | collective-permute-start | bytes 1572872 | tf_op jit(solution)/shard_map/ppermute | solution.py:24
  5.1 26.5 %copy-start = (bf16[128,2048]{1,0:T(8,128)(2,1)S(1)}, bf16[128,2048]{1,0:T(8,128)(2,1)}, u32[]{:S(2)}) copy-start(bf16[128,2048]{1,0:T(8,128)(2,1)} %q_ref.3) | copy-start | bytes 1572868
  5.1 26.5 %copy-start.1 = (bf16[128,2048]{1,0:T(8,128)(2,1)S(1)}, bf16[128,2048]{1,0:T(8,128)(2,1)}, u32[]{:S(2)}) copy-start(bf16[128,2048]{1,0:T(8,128)(2,1)} %g_ref.3) | copy-start | bytes 1572868
  5.2 26.5 %all-to-all-start = ((bf16[4,128,512]{2,1,0:T(8,128)(2,1)}), bf16[4,128,512]{2,1,0:T(8,128)(2,1)S(1)}, u32[]{:S(2)}, u32[]{:S(2)}) async-start(bf16[4,128,512]{2,1,0:T(8,128)(2,1)} %bitcast.1), calls=%async_computation | async-start | bytes 1048576 | tf_op jit(solution)/shard_map/all_to_all | solution.py:250
  21.8 9.8 %collective-permute-start.1 = (bf16[128,512]{1,0:T(8,128)(2,1)S(1)}, bf16[128,512]{1,0:T(8,128)(2,1)S(1)}, u32[]{:S(2)}, u32[]{:S(2)}) collective-permute-start(bf16[128,512]{1,0:T(8,128)(2,1)S(1)} %get-tuple-element.11.kv_ref), channel_id=1, source_target_pairs={{0,4},{4,8},{8,12},{12,16},{16,20},{20,24},{24,28},{28,32},{32,36}... | collective-permute-start | bytes 393224 | tf_op jit(solution)/shard_map/ppermute | solution.py:24
  37.3 16.4 %all-to-all-start.1 = ((bf16[4,128,512]{2,1,0:T(8,128)(2,1)}), bf16[4,128,512]{2,1,0:T(8,128)(2,1)S(1)}, u32[]{:S(2)}, u32[]{:S(2)}) async-start(bf16[4,128,512]{2,1,0:T(8,128)(2,1)} %bitcast.3), calls=%async_computation.1 | async-start | bytes 1048576 | tf_op jit(solution)/shard_map/all_to_all | solution.py:275
  42.1 11.6 %collective-permute-start.3 = (bf16[128,1024]{1,0:T(8,128)(2,1)S(1)}, bf16[128,1024]{1,0:T(8,128)(2,1)S(1)}, u32[]{:S(2)}, u32[]{:S(2)}) collective-permute-start(bf16[128,1024]{1,0:T(8,128)(2,1)S(1)} %get-tuple-element.16), channel_id=1, source_target_pairs={{0,512},{512,0},{1,513},{513,1},{2,514},{514,2},{3,515},{515,3},{4... | collective-permute-start | bytes 786440 | tf_op jit(solution)/shard_map/ppermute | solution.py:24
  45.5 8.2 %collective-permute-start.2 = (bf16[128,512]{1,0:T(8,128)(2,1)S(1)}, bf16[128,512]{1,0:T(8,128)(2,1)S(1)}, u32[]{:S(2)}, u32[]{:S(2)}) collective-permute-start(bf16[128,512]{1,0:T(8,128)(2,1)S(1)} %get-tuple-element.14), channel_id=1, source_target_pairs={{0,508},{4,0},{8,4},{12,8},{16,12},{20,16},{24,20},{28,24},{32,28}... | collective-permute-start | bytes 393224 | tf_op jit(solution)/shard_map/ppermute | solution.py:24
